TPU v7x, 256 devices: a whole 4x4x8 slice. The times are simulated.
256 devices in a mesh: dp: 32 (over z_hi, y, x), tensor: 8 (over z_lo, core).
Axes of the slice: x: 4, y: 4, z: 8 (z_hi: 2, z_lo: 4; z = z_hi * 4 + z_lo), core: 2. Of those that a mesh axis runs over, the one named last changes fastest.
Arguments:
- queries: bfloat16 [32768, 3072], P('dp', 'tensor'), may hold values from -70 to 70
- keys: bfloat16 [32768, 3072], P('dp', 'tensor'), may hold values from -5 to 5
- values: bfloat16 [32768, 3072], P('dp', 'tensor'), may hold values from -6 to 6
- out_gradient: bfloat16 [32768, 5120], P(('dp', 'tensor')), may hold values from -24 to 24
- out_weight: bfloat16 [3072, 5120], P('tensor'), may hold values from -0.109375 to 0.109375
- segments: int32 [32, 8], replicated, may hold values from 0 to 7, as said below
- counts: int32 [32], replicated, may hold values from 1 to 4, as said below
Outputs:
- query_gradient: bfloat16 [32768, 3072], P('dp', 'tensor')
- key_gradient: bfloat16 [32768, 3072], P('dp', 'tensor')
- value_gradient: bfloat16 [32768, 3072], P('dp', 'tensor')
- weight_gradient: float32 [5120, 3072], P('dp', 'tensor')
Inputs may be any that keep to these rules, and one draw needn't show every extreme that they name: `segments`: along each row ids never fall; each protein spans 1 to 4 consecutive blocks, and some protein spans exactly 4; the last counts[r] blocks of replica r are whole proteins. counts[r] equals counts[(r + 16) mod 32].
All inputs are finite; a program needn't handle non-finite values.
Results may differ from a plain program's by a relative error of at most 0.025.
Values may be sent and summed in bfloat16 or wider, within the bound.
No kernel may reach another device: no remote copies, remote signals or barrier semaphores. Data moves between devices by JAX's collectives and lax.ppermute only.
A program may use at most 128 MiB of HBM per device.

v0:
```python
import jax
import jax.numpy as jnp
from jax import lax
from jax.sharding import Mesh
from jax.sharding import PartitionSpec as P

HEAD_SIZE = 128
BLOCK = 128
DP = ("dp_0", "dp_1", "dp_2")
DP_TENSOR = ("dp_0", "dp_1", "dp_2", "tensor")
masked_score = -1e30


def swapped(x, axis, distance):
    return lax.ppermute(x, axis, [(i, i ^ 1 << distance) for i in range(lax.axis_size(axis))])


def reduced_to_own(tiles, axes, order):
    shape = [lax.axis_size(a) for a in axes]
    tiles = tiles.reshape(*shape, *tiles.shape[1:])
    tiles = tiles.transpose(*order, *range(len(axes), tiles.ndim))
    tiles = tiles.reshape(-1, *tiles.shape[len(axes) :])
    for k in order:
        tiles = lax.psum_scatter(tiles, axes[k], scatter_dimension=0, tiled=True)
    return tiles[0]


def cut_along(x, dim, devices):
    shape = x.shape
    tiles = x.reshape(*shape[:dim], devices, shape[dim] // devices, *shape[dim + 1 :])
    return jnp.moveaxis(tiles, dim, 0)


def summed_rows_2(x, axes, order, dim):
    devices = lax.axis_size(axes)
    return reduced_to_own(cut_along(x, dim, devices), axes, order)


def attend(query, key_rows, value, gradient, block_ids):
    length, inner = query.shape
    heads = inner // HEAD_SIZE
    scale = HEAD_SIZE ** (-0.5)
    total_blocks = block_ids.shape[0]
    window = total_blocks // 2

    def split(array, rows):
        return array.reshape(rows, heads, HEAD_SIZE)

    def visit(carry, index):
        key_total, value_total = carry
        own = block_ids[index]
        first = jnp.argmax(block_ids == own)
        start = jnp.minimum(first, total_blocks - window)
        query_block = split(lax.dynamic_slice_in_dim(query, index * BLOCK, BLOCK, 0), BLOCK)
        grad_block = split(lax.dynamic_slice_in_dim(gradient, index * BLOCK, BLOCK, 0), BLOCK)
        window_ids = lax.dynamic_slice_in_dim(block_ids, start, window, 0)
        key_window = split(
            lax.dynamic_slice_in_dim(key_rows, start * BLOCK, window * BLOCK, 0), window * BLOCK
        )
        value_window = split(
            lax.dynamic_slice_in_dim(value, start * BLOCK, window * BLOCK, 0), window * BLOCK
        )
        score_tiles = []
        grad_tiles = []
        for tile in range(window):
            key_tile = key_window[tile * BLOCK : (tile + 1) * BLOCK]
            value_tile = value_window[tile * BLOCK : (tile + 1) * BLOCK]

            def near(key_tile=key_tile, value_tile=value_tile):
                return (
                    jnp.einsum(
                        "qhd,khd->hqk", query_block, key_tile, preferred_element_type=jnp.float32
                    )
                    * scale,
                    jnp.einsum(
                        "qhd,khd->hqk", grad_block, value_tile, preferred_element_type=jnp.float32
                    ),
                )

            def far():
                return (
                    jnp.full((heads, BLOCK, BLOCK), masked_score, jnp.float32),
                    jnp.zeros((heads, BLOCK, BLOCK), jnp.float32),
                )

            score_tile, grad_tile = lax.cond(window_ids[tile] == own, near, far)
            score_tiles.append(score_tile)
            grad_tiles.append(grad_tile)
        scores = jnp.concatenate(score_tiles, axis=2)
        chance_gradient = jnp.concatenate(grad_tiles, axis=2)
        highest = jnp.max(scores, axis=2, keepdims=True)
        weights = jnp.exp(scores - highest)
        chances = weights / jnp.sum(weights, axis=2, keepdims=True)
        chance_weights = chances.astype(jnp.bfloat16)
        output_sum = jnp.zeros((BLOCK, heads, HEAD_SIZE), jnp.float32)
        for tile in range(window):
            value_tile = value_window[tile * BLOCK : (tile + 1) * BLOCK]
            weight_tile = chance_weights[:, :, tile * BLOCK : (tile + 1) * BLOCK]
            output_sum = output_sum + lax.cond(
                window_ids[tile] == own,
                lambda weight_tile=weight_tile, value_tile=value_tile: jnp.einsum(
                    "hqk,khd->qhd", weight_tile, value_tile, preferred_element_type=jnp.float32
                ),
                lambda: jnp.zeros((BLOCK, heads, HEAD_SIZE), jnp.float32),
            )
        head_output = output_sum.astype(jnp.bfloat16)
        centering = jnp.sum(
            grad_block.astype(jnp.float32) * head_output.astype(jnp.float32), axis=2
        )
        score_gradient = (
            chances * (chance_gradient - jnp.transpose(centering)[:, :, None])
        ).astype(jnp.bfloat16)
        query_sum = jnp.zeros((BLOCK, heads, HEAD_SIZE), jnp.float32)
        key_pieces = []
        value_pieces = []
        for tile in range(window):
            key_tile = key_window[tile * BLOCK : (tile + 1) * BLOCK]
            slope_tile = score_gradient[:, :, tile * BLOCK : (tile + 1) * BLOCK]
            weight_tile = chance_weights[:, :, tile * BLOCK : (tile + 1) * BLOCK]

            def near_back(key_tile=key_tile, slope_tile=slope_tile, weight_tile=weight_tile):
                return (
                    jnp.einsum(
                        "hqk,khd->qhd", slope_tile, key_tile, preferred_element_type=jnp.float32
                    ),
                    jnp.einsum(
                        "hqk,qhd->khd", slope_tile, query_block, preferred_element_type=jnp.float32
                    ),
                    jnp.einsum(
                        "hqk,qhd->khd", weight_tile, grad_block, preferred_element_type=jnp.float32
                    ),
                )

            def far_back():
                empty = jnp.zeros((BLOCK, heads, HEAD_SIZE), jnp.float32)
                return (empty, empty, empty)

            query_part, key_part, value_part = lax.cond(
                window_ids[tile] == own, near_back, far_back
            )
            query_sum = query_sum + query_part
            key_pieces.append(key_part.reshape(BLOCK, inner))
            value_pieces.append(value_part.reshape(BLOCK, inner))
        key_window_sum = jnp.concatenate(key_pieces, axis=0)
        value_window_sum = jnp.concatenate(value_pieces, axis=0)
        key_total = lax.dynamic_update_slice_in_dim(
            key_total,
            lax.dynamic_slice_in_dim(key_total, start * BLOCK, window * BLOCK, 0) + key_window_sum,
            start * BLOCK,
            0,
        )
        value_total = lax.dynamic_update_slice_in_dim(
            value_total,
            lax.dynamic_slice_in_dim(value_total, start * BLOCK, window * BLOCK, 0)
            + value_window_sum,
            start * BLOCK,
            0,
        )
        query_block_grad = (query_sum * scale).astype(jnp.bfloat16).reshape(BLOCK, inner)
        return ((key_total, value_total), (query_block_grad, head_output.reshape(BLOCK, inner)))

    start_totals = (
        jnp.zeros((length, inner), jnp.float32),
        jnp.zeros((length, inner), jnp.float32),
    )
    totals, stacked = lax.scan(visit, start_totals, jnp.arange(total_blocks, dtype=jnp.int32))
    query_local = stacked[0].reshape(length, inner)
    head_output = stacked[1].reshape(length, inner)
    key_local = (totals[0] * scale).astype(jnp.bfloat16)
    value_local = totals[1].astype(jnp.bfloat16)
    return (query_local, key_local, value_local, head_output)


def shards(queries, keys, values, out_gradient, out_weight, segments, counts):
    full_gradient = lax.all_gather(out_gradient, "tensor", axis=0, tiled=True)
    head_gradient = lax.dot_general(
        full_gradient, out_weight, (((1,), (1,)), ((), ())), preferred_element_type=jnp.float32
    ).astype(jnp.bfloat16)
    replicas = lax.axis_size(DP)
    halfway = replicas // 2
    position = lax.axis_index(DP)
    blocks = segments.shape[1]
    block_rows = queries.shape[0] // blocks
    trailing = blocks // 2 * block_rows
    moving = lax.dynamic_index_in_dim(counts, position, 0, keepdims=False)
    own_blocks = lax.dynamic_index_in_dim(segments, position, 0, keepdims=False)
    block_moved = jnp.arange(blocks, dtype=jnp.int32) >= blocks - moving
    row_moved = jnp.repeat(block_moved, block_rows)[-trailing:, None]
    flip_bit = halfway.bit_length() - 1

    def settle(local, arrived):
        upper = jnp.where(row_moved, arrived, local[-trailing:])
        return jnp.concatenate([local[:-trailing], upper], axis=0)

    query_local, key_local, value_local, head_output = attend(
        queries, keys, values, head_gradient, own_blocks
    )
    arrived = swapped(
        (query_local[-trailing:], key_local[-trailing:], value_local[-trailing:]), DP, flip_bit
    )
    query_gradient = settle(query_local, arrived[0])
    key_gradient = settle(key_local, arrived[1])
    value_gradient = settle(value_local, arrived[2])
    weight_gradient = summed_rows_2(
        lax.dot_general(
            full_gradient, head_output, (((0,), (0,)), ((), ())), preferred_element_type=jnp.float32
        )
        / replicas,
        DP,
        (1, 2, 0),
        0,
    )
    return (query_gradient, key_gradient, value_gradient, weight_gradient)


def solution(mesh):
    split = Mesh(
        mesh.devices.reshape(2, 4, 4, mesh.shape["tensor"]), ("dp_0", "dp_1", "dp_2", "tensor")
    )
    placed = (
        P(DP, "tensor"),
        P(DP, "tensor"),
        P(DP, "tensor"),
        P(DP_TENSOR, None),
        P("tensor", None),
        P(),
        P(),
    )
    return jax.shard_map(
        shards,
        mesh=split,
        in_specs=placed,
        out_specs=(P(DP, "tensor"), P(DP, "tensor"), P(DP, "tensor"), P(DP, "tensor")),
        check_vma=False,
    )
```

profile of v0, /device:TPU:1, one launch (start us, length us, event | category | flops | bytes accessed | tf_op | source)
XLA Modules:
  0.0 550.3 jit_solution(16349101674922859828)
XLA Ops:
  8.2 116.8 %all-gather.2.cloned.1.call-done = bf16[1024,5120]{1,0:T(8,128)(2,1)} async-done(((bf16[128,5120]{1,0:T(8,128)(2,1)}), bf16[1024,5120]{1,0:T(8,128)(2,1)}) %all-gather.2.cloned.1.call-update) | async-done | bytes 10485776 | tf_op jit(solution)/shard_map/all_gather | solution.py:175
  125.0 9.5 %convolution_convert_fusion = bf16[1024,384]{1,0:T(8,128)(2,1)S(1)} fusion(bf16[1024,5120]{1,0:T(8,128)(2,1)} %all-gather.2.cloned.1.call-done, bf16[384,5120]{1,0:T(8,128)(2,1)} %param.37), kind=kOutput, calls=%fused_computation.57 | convolution fusion | flops 4026925056 | bytes 15204352 | tf_op jit(solution)/shard_map/dot_general | solution.py:176
  137.0 223.8 %while.16 = (s32[]{:T(128)}, f32[1024,384]{1,0:T(8,128)}, f32[1024,384]{1,0:T(8,128)}, bf16[8,128,384]{1,2,0:T(8,128)(2,1)}, bf16[8,128,384]{2,1,0:T(8,128)(2,1)...) while((s32[]{:T(128)}, f32[1024,384]{1,0:T(8,128)}, ...), condition=%wide.region_32.33_spmd, body=%wide.region_0.32_spmd.sunk | while | flops 308919232 | bytes 47705920 | solution.py:166
  157.0 1.5 constant_dynamic-slice_fusion.15
  183.4 1.5 constant_dynamic-slice_fusion.15
  195.1 1.3 constant_dynamic-slice_fusion.17
  209.8 1.5 constant_dynamic-slice_fusion.15
  236.2 1.5 constant_dynamic-slice_fusion.15
  247.9 1.3 constant_dynamic-slice_fusion.17
  265.8 1.5 constant_dynamic-slice_fusion.15
  295.3 1.5 constant_dynamic-slice_fusion.15
  324.9 1.5 constant_dynamic-slice_fusion.15
  354.4 1.5 constant_dynamic-slice_fusion.15
  360.9 11.7 %multiply_bitcast_fusion = f32[5120,384]{0,1:T(8,128)} fusion(bf16[1024,384]{1,0:T(8,128)(2,1)} %bitcast.202, bf16[1024,5120]{1,0:T(8,128)(2,1)} %all-gather.2.cloned.1.call-done), kind=kOutput, calls=%fused_computation.55 | convolution fusion | flops 4028497920 | bytes 19136512 | tf_op jit(solution)/shard_map/dot_general | solution.py:205
  372.6 9.1 %copy.87 = f32[5120,384]{1,0:T(8,128)} copy(f32[5120,384]{0,1:T(8,128)} %multiply_bitcast_fusion) | data formatting | bytes 15728640 | tf_op jit(solution)/shard_map/div | solution.py:205
  381.7 7.1 %copy.88 = f32[4,4,2,160,384]{4,3,2,1,0:T(8,128)} copy(f32[4,4,2,160,384]{4,3,1,0,2:T(8,128)} %bitcast.173) | data formatting | bytes 15728640 | tf_op jit(solution)/shard_map/transpose | solution.py:21
  388.9 82.4 %reduce-scatter.4.cloned.1.call-done = f32[8,160,384]{2,1,0:T(8,128)} async-done(((f32[32,160,384]{2,1,0:T(8,128)}), f32[8,160,384]{2,1,0:T(8,128)}) %reduce-scatter.4.cloned.1.call-update) | async-done | bytes 1966096 | tf_op jit(solution)/shard_map/reduce_scatter | solution.py:24
  471.7 5.5 %collective-permute-start = (bf16[512,384]{1,0:T(8,128)(2,1)S(1)}, bf16[512,384]{1,0:T(8,128)(2,1)}, u32[]{:S(2)}, u32[]{:S(2)}) collective-permute-start(bf16[512,384]{1,0:T(8,128)(2,1)S(1)} %bitcast.201), channel_id=1, source_target_pairs={{0,128},{8,136},{16,144},{24,152},{32,160},{40,168},{48,176},{56,1... | collective-permute-start | bytes 1179656 | tf_op jit(solution)/shard_map/ppermute | solution.py:15
  477.2 1.7 multiply_convert_fusion.1
  479.3 5.4 collective-permute-start.2
  485.9 19.0 %reduce-scatter.6.cloned.1.call-done = f32[2,160,384]{2,1,0:T(8,128)} async-done(((f32[8,160,384]{2,1,0:T(8,128)}), f32[2,160,384]{2,1,0:T(8,128)}) %reduce-scatter.6.cloned.1.call-update) | async-done | bytes 491536 | tf_op jit(solution)/shard_map/reduce_scatter | solution.py:24
  505.3 11.7 %collective-permute-done.2 = bf16[512,384]{1,0:T(8,128)(2,1)} collective-permute-done((bf16[512,384]{1,0:T(8,128)(2,1)S(1)}, bf16[512,384]{1,0:T(8,128)(2,1)}, u32[]{:S(2)}, u32[]{:S(2)}) %collective-permute-start.2) | collective-permute-done | bytes 393248 | tf_op jit(solution)/shard_map/ppermute | solution.py:15
  517.0 1.5 fusion.19
  521.4 22.3 %reduce-scatter.8.cloned.1.call-done = f32[1,160,384]{2,1,0:T(8,128)} async-done(((f32[2,160,384]{2,1,0:T(8,128)}), f32[1,160,384]{2,1,0:T(8,128)}) %reduce-scatter.8.cloned.1.call-update) | async-done | bytes 245776 | tf_op jit(solution)/shard_map/reduce_scatter | solution.py:24
  (734 shorter events, 172.6 us)
Async XLA Ops:
  7.2 117.9 %all-gather.2.cloned.1.call-start = ((), (), s32[]{:S(2)}) async-start(), calls=%async_computation.3 | async-start | bytes 11796480 | tf_op jit(solution)/shard_map/all_gather | solution.py:175
  7.9 463.4 %reduce-scatter.4.cloned.1.call-start = ((), (), s32[]{:S(2)}) async-start(), calls=%async_computation.4 | async-start | bytes 9830400 | tf_op jit(solution)/shard_map/reduce_scatter | solution.py:24
  137.0 10.6 %copy-start.8 = (bf16[1024,384]{1,0:T(8,128)(2,1)}, bf16[1024,384]{1,0:T(8,128)(2,1)S(1)}, u32[]{:S(2)}) copy-start(bf16[1024,384]{1,0:T(8,128)(2,1)S(1)} %get-tuple-element.628) | copy-start | bytes 2359300 | tf_op jit(solution)/shard_map/while
  163.5 10.6 %copy-start.8 = (bf16[1024,384]{1,0:T(8,128)(2,1)}, bf16[1024,384]{1,0:T(8,128)(2,1)S(1)}, u32[]{:S(2)}) copy-start(bf16[1024,384]{1,0:T(8,128)(2,1)S(1)} %get-tuple-element.628) | copy-start | bytes 2359300 | tf_op jit(solution)/shard_map/while
  182.7 2.2 copy-start.3
  189.9 10.6 %copy-start.8 = (bf16[1024,384]{1,0:T(8,128)(2,1)}, bf16[1024,384]{1,0:T(8,128)(2,1)S(1)}, u32[]{:S(2)}) copy-start(bf16[1024,384]{1,0:T(8,128)(2,1)S(1)} %get-tuple-element.628) | copy-start | bytes 2359300 | tf_op jit(solution)/shard_map/while
  209.1 2.2 copy-start.3
  216.3 10.6 %copy-start.8 = (bf16[1024,384]{1,0:T(8,128)(2,1)}, bf16[1024,384]{1,0:T(8,128)(2,1)S(1)}, u32[]{:S(2)}) copy-start(bf16[1024,384]{1,0:T(8,128)(2,1)S(1)} %get-tuple-element.628) | copy-start | bytes 2359300 | tf_op jit(solution)/shard_map/while
  235.5 2.2 copy-start.3
  242.7 10.6 %copy-start.8 = (bf16[1024,384]{1,0:T(8,128)(2,1)}, bf16[1024,384]{1,0:T(8,128)(2,1)S(1)}, u32[]{:S(2)}) copy-start(bf16[1024,384]{1,0:T(8,128)(2,1)S(1)} %get-tuple-element.628) | copy-start | bytes 2359300 | tf_op jit(solution)/shard_map/while
  265.0 2.2 copy-start.3
  272.2 10.6 %copy-start.8 = (bf16[1024,384]{1,0:T(8,128)(2,1)}, bf16[1024,384]{1,0:T(8,128)(2,1)S(1)}, u32[]{:S(2)}) copy-start(bf16[1024,384]{1,0:T(8,128)(2,1)S(1)} %get-tuple-element.628) | copy-start | bytes 2359300 | tf_op jit(solution)/shard_map/while
  301.8 10.6 %copy-start.8 = (bf16[1024,384]{1,0:T(8,128)(2,1)}, bf16[1024,384]{1,0:T(8,128)(2,1)S(1)}, u32[]{:S(2)}) copy-start(bf16[1024,384]{1,0:T(8,128)(2,1)S(1)} %get-tuple-element.628) | copy-start | bytes 2359300 | tf_op jit(solution)/shard_map/while
  324.1 2.2 copy-start.3
  331.3 10.6 %copy-start.8 = (bf16[1024,384]{1,0:T(8,128)(2,1)}, bf16[1024,384]{1,0:T(8,128)(2,1)S(1)}, u32[]{:S(2)}) copy-start(bf16[1024,384]{1,0:T(8,128)(2,1)S(1)} %get-tuple-element.628) | copy-start | bytes 2359300 | tf_op jit(solution)/shard_map/while
  353.7 2.2 copy-start.3
  388.8 82.6 %copy-start.7 = (bf16[8,128,384]{1,2,0:T(8,128)(2,1)S(1)}, bf16[8,128,384]{1,2,0:T(8,128)(2,1)}, u32[]{:S(2)}) copy-start(bf16[8,128,384]{1,2,0:T(8,128)(2,1)} %get-tuple-element.241) | copy-start | bytes 2359300
  388.8 116.0 %reduce-scatter.6.cloned.1.call-start = ((), (), s32[]{:S(2)}) async-start(), calls=%async_computation.5 | async-start | bytes 2457600 | tf_op jit(solution)/shard_map/reduce_scatter | solution.py:24
  471.4 72.4 %reduce-scatter.8.cloned.1.call-start = ((), (), s32[]{:S(2)}) async-start(), calls=%async_computation.6 | async-start | bytes 737280 | tf_op jit(solution)/shard_map/reduce_scatter | solution.py:24
  471.7 33.6 %collective-permute-start = (bf16[512,384]{1,0:T(8,128)(2,1)S(1)}, bf16[512,384]{1,0:T(8,128)(2,1)}, u32[]{:S(2)}, u32[]{:S(2)}) collective-permute-start(bf16[512,384]{1,0:T(8,128)(2,1)S(1)} %bitcast.201), channel_id=1, source_target_pairs={{0,128},{8,136},{16,144},{24,152},{32,160},{40,168},{48,176},{56,1... | collective-permute-start | bytes 1179656 | tf_op jit(solution)/shard_map/ppermute | solution.py:15
  479.0 26.3 %collective-permute-start.1 = (bf16[512,384]{1,0:T(8,128)(2,1)S(1)}, bf16[512,384]{1,0:T(8,128)(2,1)}, u32[]{:S(2)}, u32[]{:S(2)}) collective-permute-start(bf16[512,384]{1,0:T(8,128)(2,1)S(1)} %slice.154), channel_id=1, source_target_pairs={{0,128},{8,136},{16,144},{24,152},{32,160},{40,168},{48,176},{56,1... | collective-permute-start | bytes 1179656 | tf_op jit(solution)/shard_map/ppermute | solution.py:15
  479.1 5.5 %copy-start.10 = (s32[32]{0:T(128)S(1)}, s32[32]{0:T(128)}, u32[]{:S(2)}) copy-start(s32[32]{0:T(128)} %param.39) | copy-start | bytes 388
  479.3 37.8 %collective-permute-start.2 = (bf16[512,384]{1,0:T(8,128)(2,1)S(1)}, bf16[512,384]{1,0:T(8,128)(2,1)}, u32[]{:S(2)}, u32[]{:S(2)}) collective-permute-start(bf16[512,384]{1,0:T(8,128)(2,1)S(1)} %slice.156), channel_id=1, source_target_pairs={{0,128},{8,136},{16,144},{24,152},{32,160},{40,168},{48,176},{56,1... | collective-permute-start | bytes 1179656 | tf_op jit(solution)/shard_map/ppermute | solution.py:15
  519.5 24.2 %copy-start.1 = (s32[32,8]{0,1:T(8,128)S(1)}, s32[32,8]{0,1:T(8,128)}, u32[]{:S(2)}) copy-start(s32[32,8]{0,1:T(8,128)} %param.38) | copy-start | bytes 3076
  (36 other events, 61.0 us)
Sparse Core Ops, SparseCore 0:
  9.8 115.2 all-gather.1
  388.9 82.3 reduce-scatter.3
  473.9 30.9 reduce-scatter.5
  507.8 35.8 reduce-scatter.7
where the time goes:
time: 553 us; the launch traced here: 550 us
  waiting for transfers between devices  253 us (46%)
  local copies, waits for them, and re-layouts  113 us (20%)
  loops' own time  71.5 us (13%)
  matrix products  44.1 us (8%)
  other arithmetic  42.3 us (8%)
  between operations  14.6 us (3%)
  starting transfers between devices  11.2 us (2%)
    reduce_scatter x3, waiting for transfers between devices, reduced_to_own(): tiles = lax.psum_scatter(tiles, axes[k], scatter_dimension=0, tiled=True)  124 us
    all_gather x1, waiting for transfers between devices, shards(): full_gradient = lax.all_gather(out_gradient, 'tensor', axis=0, tiled=True)  117 us
    another operation x1, loops' own time, attend(): lax.scan(visit, start_totals, jnp.arange(total_blocks, dtype=jnp.int32))  68.9 us
    dynamic_slice x16, local copies, waits for them, and re-layouts, visit(): lax.dynamic_slice_in_dim(value_total, start * BLOCK, window * BLOCK, 0)  13.9 us
    dynamic_update_slice x24, local copies, waits for them, and re-layouts, attend(): lax.scan(visit, start_totals, jnp.arange(total_blocks, dtype=jnp.int32))  11.8 us
    dot_general x1, matrix products, shards(): lax.dot_general(full_gradient, head_output, (((0,), (0,)), ((), ())), pre...  11.7 us
    ppermute x3, waiting for transfers between devices, swapped(): lax.ppermute(x, axis, [(i, i ^ 1 << distance) for i in range(lax.axis_siz...  11.7 us
    ppermute x3, starting transfers between devices, swapped(): lax.ppermute(x, axis, [(i, i ^ 1 << distance) for i in range(lax.axis_siz...  11.1 us
  transfers between devices with their start and end apart: 7, of which 5 were waited for; matrix products, arithmetic and copies ran while one was open for 1% of the time, Pallas kernels for 0%

commit v1 on v0

--- a/solution.py
+++ b/solution.py
@@ -172,7 +172,15 @@
 
 
 def shards(queries, keys, values, out_gradient, out_weight, segments, counts):
-    full_gradient = lax.all_gather(out_gradient, "tensor", axis=0, tiled=True)
+    full_gradient = jnp.concatenate(
+        lax.all_to_all(
+            jnp.stack(lax.axis_size("tensor") * [out_gradient], axis=0),
+            axis_name="tensor",
+            split_axis=0,
+            concat_axis=0,
+        ),
+        axis=0,
+    )
     head_gradient = lax.dot_general(
         full_gradient, out_weight, (((1,), (1,)), ((), ())), preferred_element_type=jnp.float32
     ).astype(jnp.bfloat16)

time: 553 us -> 840 us (1.52)
  waiting for transfers between devices: 253 us -> 379 us
  local copies, waits for them, and re-layouts: 113 us -> 180 us
  matrix products: 44.1 us -> 108 us
  other arithmetic: 42.3 us -> 61.3 us
    all_to_all x0 -> x1, waiting for transfers between devices: none -> 228 us  [shards(): lax.all_to_all(jnp.stack(lax.axis_size('tensor') * [out_gradient], axis=0...]
    all_gather x1 -> x0, waiting for transfers between devices: 117 us -> none  [shards(): full_gradient = lax.all_gather(out_gradient, 'tensor', axis=0, tiled=True)]
    while x160 -> x384, local copies, waits for them, and re-layouts: 8.24 us -> 63.5 us
    dot_general x20, matrix products: 3.8 us -> 27.2 us  [visit(): jnp.einsum('hqk,khd->qhd', weight_tile, value_tile, preferred_element_typ...]
    dot_general x20, matrix products: 4.4 us -> 22.3 us  [near(): jnp.einsum('qhd,khd->hqk', grad_block, value_tile, preferred_element_type...]
    reduce_scatter x3, waiting for transfers between devices: 124 us -> 139 us  [reduced_to_own(): tiles = lax.psum_scatter(tiles, axes[k], scatter_dimension=0, tiled=True)]
    another operation x50 -> x51, local copies, waits for them, and re-layouts: 3.23 us -> 14.2 us
    dot_general x20, matrix products: 3.91 us -> 14.6 us  [near_back(): jnp.einsum('hqk,khd->qhd', slope_tile, key_tile, preferred_element_type=j...]
where the time goes in v1:
time: 840 us; the launch traced here: 834 us
  waiting for transfers between devices  379 us (45%)
  local copies, waits for them, and re-layouts  180 us (21%)
  matrix products  108 us (13%)
  loops' own time  71.6 us (9%)
  other arithmetic  61.3 us (7%)
  starting transfers between devices  19.4 us (2%)
  between operations  14.5 us (2%)
    all_to_all x1, waiting for transfers between devices, shards(): lax.all_to_all(jnp.stack(lax.axis_size('tensor') * [out_gradient], axis=0...  228 us
    reduce_scatter x3, waiting for transfers between devices, reduced_to_own(): tiles = lax.psum_scatter(tiles, axes[k], scatter_dimension=0, tiled=True)  139 us
    another operation x1, loops' own time, attend(): lax.scan(visit, start_totals, jnp.arange(total_blocks, dtype=jnp.int32))  69.4 us
    while x384, local copies, waits for them, and re-layouts  63.5 us
    dot_general x20, matrix products, visit(): jnp.einsum('hqk,khd->qhd', weight_tile, value_tile, preferred_element_typ...  27.2 us
    dot_general x20, matrix products, near(): jnp.einsum('qhd,khd->hqk', grad_block, value_tile, preferred_element_type...  22.3 us
  transfers between devices with their start and end apart: 7, of which 5 were waited for; matrix products, arithmetic and copies ran while one was open for 1% of the time, Pallas kernels for 0%

profile of v1, /device:TPU:1, one launch (start us, length us, event | category | flops | bytes accessed | tf_op | source)
XLA Modules:
  0.0 834.0 jit_solution(5396223296286677592)
XLA Ops:
  7.2 6.6 stack.2
  13.8 8.2 all-to-all-start
  22.2 227.8 %all-to-all-done = bf16[8,128,5120]{2,1,0:T(8,128)(2,1)} async-done(((bf16[8,128,5120]{2,1,0:T(8,128)(2,1)}), bf16[8,128,5120]{2,1,0:T(8,128)(2,1)}, u32[]{:S(2)}, u32[]{:S(2)}) %all-to-all-start) | async-done | bytes 10485792 | tf_op jit(solution)/shard_map/all_to_all | solution.py:176
  250.0 10.2 %convolution_convert_fusion = bf16[1024,384]{1,0:T(8,128)(2,1)} fusion(bf16[1024,5120]{1,0:T(8,128)(2,1)} %bitcast.43, bf16[384,5120]{1,0:T(8,128)(2,1)} %param.37), kind=kOutput, calls=%fused_computation.58 | convolution fusion | flops 4026925056 | bytes 15204352 | tf_op jit(solution)/shard_map/dot_general | solution.py:184
  261.6 368.1 %while.16 = (s32[]{:T(128)}, f32[1024,384]{1,0:T(8,128)}, f32[1024,384]{1,0:T(8,128)S(1)}, bf16[8,128,384]{1,2,0:T(8,128)(2,1)}, bf16[8,128,384]{1,2,0:T(8,128)(...) while((s32[]{:T(128)}, f32[1024,384]{1,0:T(8,128)}, ...), condition=%wide.region_32.33_spmd, body=%wide.region_0.32_spmd.sunk | while | flops 308919232 | bytes 64811208 | solution.py:166
  278.3 2.3 conditional.27
  360.0 2.3 conditional.27
  444.3 2.3 conditional.27
  449.5 2.3 conditional.26
  495.5 2.3 conditional.27
  500.6 2.3 conditional.26
  546.6 2.3 conditional.27
  551.8 2.3 conditional.26
  597.8 2.3 conditional.27
  602.9 2.3 conditional.26
  629.6 9.0 %fusion.17 = f32[5120,384]{0,1:T(8,128)} fusion(bf16[8,128,384]{1,2,0:T(8,128)(2,1)} %get-tuple-element.244, bf16[8,128,5120]{2,1,0:T(8,128)(2,1)} %all-to-all-done), kind=kOutput, calls=%fused_computation.56 | convolution fusion | flops 4028497920 | bytes 19136512 | tf_op jit(solution)/shard_map/dot_general | solution.py:213
  638.6 9.1 %copy.85 = f32[5120,384]{1,0:T(8,128)} copy(f32[5120,384]{0,1:T(8,128)} %fusion.17) | data formatting | bytes 15728640 | tf_op jit(solution)/shard_map/div | solution.py:213
  647.7 7.1 copy.86
  654.9 99.2 %reduce-scatter.4.cloned.1.call-done = f32[8,160,384]{2,1,0:T(8,128)} async-done(((f32[32,160,384]{2,1,0:T(8,128)}), f32[8,160,384]{2,1,0:T(8,128)}) %reduce-scatter.4.cloned.1.call-update) | async-done | bytes 1966096 | tf_op jit(solution)/shard_map/reduce_scatter | solution.py:24
  755.3 5.4 collective-permute-start
  763.2 5.5 collective-permute-start.2
  769.9 17.6 %reduce-scatter.6.cloned.1.call-done = f32[2,160,384]{2,1,0:T(8,128)} async-done(((f32[8,160,384]{2,1,0:T(8,128)}), f32[2,160,384]{2,1,0:T(8,128)}) %reduce-scatter.6.cloned.1.call-update) | async-done | bytes 491536 | tf_op jit(solution)/shard_map/reduce_scatter | solution.py:24
  788.0 12.9 %collective-permute-done.2 = bf16[512,384]{1,0:T(8,128)(2,1)} collective-permute-done((bf16[512,384]{1,0:T(8,128)(2,1)S(1)}, bf16[512,384]{1,0:T(8,128)(2,1)}, u32[]{:S(2)}, u32[]{:S(2)}) %collective-permute-start.2) | collective-permute-done | bytes 393248 | tf_op jit(solution)/shard_map/ppermute | solution.py:15
  805.5 21.9 %reduce-scatter.8.cloned.1.call-done = f32[1,160,384]{2,1,0:T(8,128)} async-done(((f32[2,160,384]{2,1,0:T(8,128)}), f32[1,160,384]{2,1,0:T(8,128)}) %reduce-scatter.8.cloned.1.call-update) | async-done | bytes 245776 | tf_op jit(solution)/shard_map/reduce_scatter | solution.py:24
  (948 shorter events, 384.6 us)
Async XLA Ops:
  7.2 14.9 %copy-start = (s32[32,8]{0,1:T(8,128)S(1)}, s32[32,8]{0,1:T(8,128)}, u32[]{:S(2)}) copy-start(s32[32,8]{0,1:T(8,128)} %param.38) | copy-start | bytes 3076
  13.8 236.2 %all-to-all-start = ((bf16[8,128,5120]{2,1,0:T(8,128)(2,1)}), bf16[8,128,5120]{2,1,0:T(8,128)(2,1)}, u32[]{:S(2)}, u32[]{:S(2)}) async-start(bf16[8,128,5120]{2,1,0:T(8,128)(2,1)} %stack.2), calls=%async_computation | async-start | bytes 20971520 | tf_op jit(solution)/shard_map/all_to_all | solution.py:176
  22.0 732.0 %reduce-scatter.4.cloned.1.call-start = ((), (), s32[]{:S(2)}) async-start(), calls=%async_computation.4 | async-start | bytes 9830400 | tf_op jit(solution)/shard_map/reduce_scatter | solution.py:24
  261.6 33.6 %copy-start.2 = (f32[1024,384]{1,0:T(8,128)}, f32[1024,384]{1,0:T(8,128)S(1)}, u32[]{:S(2)}) copy-start(f32[1024,384]{1,0:T(8,128)S(1)} %get-tuple-element.600) | copy-start | bytes 4718596 | tf_op jit(solution)/shard_map/while
  280.5 3.1 copy-start.19
  302.5 33.6 %copy-start.2 = (f32[1024,384]{1,0:T(8,128)}, f32[1024,384]{1,0:T(8,128)S(1)}, u32[]{:S(2)}) copy-start(f32[1024,384]{1,0:T(8,128)S(1)} %get-tuple-element.600) | copy-start | bytes 4718596 | tf_op jit(solution)/shard_map/while
  343.3 33.6 %copy-start.2 = (f32[1024,384]{1,0:T(8,128)}, f32[1024,384]{1,0:T(8,128)S(1)}, u32[]{:S(2)}) copy-start(f32[1024,384]{1,0:T(8,128)S(1)} %get-tuple-element.600) | copy-start | bytes 4718596 | tf_op jit(solution)/shard_map/while
  384.2 33.6 %copy-start.2 = (f32[1024,384]{1,0:T(8,128)}, f32[1024,384]{1,0:T(8,128)S(1)}, u32[]{:S(2)}) copy-start(f32[1024,384]{1,0:T(8,128)S(1)} %get-tuple-element.600) | copy-start | bytes 4718596 | tf_op jit(solution)/shard_map/while
  425.0 43.9 %copy-start.2 = (f32[1024,384]{1,0:T(8,128)}, f32[1024,384]{1,0:T(8,128)S(1)}, u32[]{:S(2)}) copy-start(f32[1024,384]{1,0:T(8,128)S(1)} %get-tuple-element.600) | copy-start | bytes 4718596 | tf_op jit(solution)/shard_map/while
  446.6 5.3 copy-start.19
  476.2 43.9 %copy-start.2 = (f32[1024,384]{1,0:T(8,128)}, f32[1024,384]{1,0:T(8,128)S(1)}, u32[]{:S(2)}) copy-start(f32[1024,384]{1,0:T(8,128)S(1)} %get-tuple-element.600) | copy-start | bytes 4718596 | tf_op jit(solution)/shard_map/while
  497.7 5.3 copy-start.19
  527.3 43.9 %copy-start.2 = (f32[1024,384]{1,0:T(8,128)}, f32[1024,384]{1,0:T(8,128)S(1)}, u32[]{:S(2)}) copy-start(f32[1024,384]{1,0:T(8,128)S(1)} %get-tuple-element.600) | copy-start | bytes 4718596 | tf_op jit(solution)/shard_map/while
  548.9 5.3 copy-start.19
  578.5 43.9 %copy-start.2 = (f32[1024,384]{1,0:T(8,128)}, f32[1024,384]{1,0:T(8,128)S(1)}, u32[]{:S(2)}) copy-start(f32[1024,384]{1,0:T(8,128)S(1)} %get-tuple-element.600) | copy-start | bytes 4718596 | tf_op jit(solution)/shard_map/while
  600.0 5.3 copy-start.19
  654.8 99.5 %copy-start.22 = (bf16[8,128,384]{1,2,0:T(8,128)(2,1)S(1)}, bf16[8,128,384]{1,2,0:T(8,128)(2,1)}, u32[]{:S(2)}) copy-start(bf16[8,128,384]{1,2,0:T(8,128)(2,1)} %get-tuple-element.241) | copy-start | bytes 2359300
  654.8 132.8 %reduce-scatter.6.cloned.1.call-start = ((), (), s32[]{:S(2)}) async-start(), calls=%async_computation.5 | async-start | bytes 2457600 | tf_op jit(solution)/shard_map/reduce_scatter | solution.py:24
  754.1 73.4 %reduce-scatter.8.cloned.1.call-start = ((), (), s32[]{:S(2)}) async-start(), calls=%async_computation.6 | async-start | bytes 737280 | tf_op jit(solution)/shard_map/reduce_scatter | solution.py:24
  755.3 32.7 %collective-permute-start = (bf16[512,384]{1,0:T(8,128)(2,1)}, bf16[512,384]{1,0:T(8,128)(2,1)}, u32[]{:S(2)}, u32[]{:S(2)}) collective-permute-start(bf16[512,384]{1,0:T(8,128)(2,1)} %bitcast.47), channel_id=1, source_target_pairs={{0,128},{8,136},{16,144},{24,152},{32,160},{40,168},{48,176},{56,1... | collective-permute-start | bytes 1179656 | tf_op jit(solution)/shard_map/ppermute | solution.py:15
  763.1 24.9 %collective-permute-start.1 = (bf16[512,384]{1,0:T(8,128)(2,1)}, bf16[512,384]{1,0:T(8,128)(2,1)}, u32[]{:S(2)}, u32[]{:S(2)}) collective-permute-start(bf16[512,384]{1,0:T(8,128)(2,1)} %slice.154), channel_id=1, source_target_pairs={{0,128},{8,136},{16,144},{24,152},{32,160},{40,168},{48,176},{56,1... | collective-permute-start | bytes 1179656 | tf_op jit(solution)/shard_map/ppermute | solution.py:15
  763.1 5.6 copy-start.23
  763.2 37.7 %collective-permute-start.2 = (bf16[512,384]{1,0:T(8,128)(2,1)S(1)}, bf16[512,384]{1,0:T(8,128)(2,1)}, u32[]{:S(2)}, u32[]{:S(2)}) collective-permute-start(bf16[512,384]{1,0:T(8,128)(2,1)S(1)} %slice.156), channel_id=1, source_target_pairs={{0,128},{8,136},{16,144},{24,152},{32,160},{40,168},{48,176},{56,1... | collective-permute-start | bytes 1179656 | tf_op jit(solution)/shard_map/ppermute | solution.py:15
  803.6 23.8 %copy-start.1 = (s32[32,8]{0,1:T(8,128)S(1)}, s32[32,8]{0,1:T(8,128)}, u32[]{:S(2)}) copy-start(s32[32,8]{0,1:T(8,128)} %param.38) | copy-start | bytes 3076
  (147 other events, 186.0 us)
Sparse Core Ops, SparseCore 0:
  654.9 99.1 reduce-scatter.3
  756.6 30.8 reduce-scatter.5
  790.7 36.7 reduce-scatter.7
